TPU v7x, 512 devices: a whole 4x4x16 slice. The times are simulated.
512 devices in a mesh: rep: 8 (over x_lo, y), fsdp: 64 (over z, x_hi, core).
Axes of the slice: x: 4 (x_hi: 2, x_lo: 2; x = x_hi * 2 + x_lo), y: 4, z: 16, core: 2. Of those that a mesh axis runs over, the one named last changes fastest.
Arguments:
- tracker: bfloat16 [8, 64, 128, 5120], P('rep', None, 'fsdp'), may hold values from -40 to 40
- levels: bfloat16 [8, 64, 128, 5120], P('rep', None, 'fsdp'), may hold values from -127 to 127, as said below
- exponents: int32 [8, 64, 128], P('rep', None, 'fsdp'), may hold values from -8 to -5
Outputs:
- update: bfloat16 [8, 64, 128, 5120], P('rep', None, 'fsdp')
Inputs may be any that keep to these rules, and one draw needn't show every extreme that they name: `levels`: whole numbers.
All inputs are finite; a program needn't handle non-finite values.
Results may differ from a plain program's by a relative error of at most 0.025.
Values may be sent and summed in bfloat16 or wider, within the bound.
A program may use at most 64 MiB of HBM per device.

v0:
```python
import functools
import math

import jax
import jax.numpy as jnp
from jax import lax
from jax.experimental import pallas as pl
from jax.experimental.pallas import tpu as pltpu
from jax.sharding import PartitionSpec as P

NS_STEPS = 5
CHUNKS = 5
MESH = pl.DeviceIdType.MESH

gamma_mix = 0.5
coef_a = 3.4445
coef_b = -4.775
coef_c = 2.0315


def dot32(a, b):
    return lax.dot_general(
        a, b, (((1,), (0,)), ((), ())),
        precision=lax.Precision.HIGHEST, preferred_element_type=jnp.float32,
    )


def newton_schulz_factor(gram, columns):
    size = gram.shape[0]
    row = lax.broadcasted_iota(jnp.int32, (size, size), 0)
    col = lax.broadcasted_iota(jnp.int32, (size, size), 1)
    eye = row == col
    total = jnp.sum(jnp.sum(jnp.where(eye, gram, 0.0), axis=1, keepdims=True), axis=0, keepdims=True)
    scale = 1.0 / (jnp.sqrt(total) + 1e-07)
    gram = (gram * scale) * scale
    factor = None
    for step in range(NS_STEPS):
        square = dot32(gram, gram)
        poly = jnp.where(eye, coef_a, 0.0) + coef_b * gram + coef_c * square
        factor = poly if factor is None else dot32(poly, factor)
        if step < NS_STEPS - 1:
            gram = dot32(dot32(poly, gram), poly)
    return factor * (scale * 2.0 ** (int(math.log2(columns)) // 2))


def kernel(
    reps, owners, columns, tracker, levels, powers, out,
    message, from_left, from_right, mixed, held, done,
    gossip_send, gossip_recv, in_send, in_recv, out_send, out_recv, own_sem,
):
    rep, me = lax.axis_index("rep"), lax.axis_index("fsdp")
    after, before = lax.rem(rep + 1, reps), lax.rem(rep + reps - 1, reps)
    width = columns // CHUNKS
    rows = 2 * owners

    barrier = pltpu.get_barrier_semaphore()

    def greet(k, carry):
        pl.semaphore_signal(
            barrier, inc=1, device_id=(rep, lax.rem(me + k, owners)), device_id_type=MESH
        )
        return carry

    for other in (before, after):
        pl.semaphore_signal(barrier, inc=1, device_id=(other, me), device_id_type=MESH)
    lax.fori_loop(1, owners, greet, 0)

    def span(c):
        return slice(c * width, (c + 1) * width)

    for c in range(CHUNKS):
        message[c] = levels[:, :, span(c)] * powers[...]
    pl.semaphore_wait(barrier, owners + 1)

    gossip = []
    for c in range(CHUNKS):
        pair = []
        for side, (other, landing) in enumerate(((after, from_left), (before, from_right))):
            copy = pltpu.make_async_remote_copy(
                message.at[c], landing.at[c], gossip_send.at[side, c], gossip_recv.at[side, c],
                device_id=(other, me), device_id_type=MESH,
            )
            copy.start()
            pair.append(copy)
        gossip.append(pair)

    def exchange(source, landing, send_sem, recv_sem):
        def send(k, carry):
            peer = lax.rem(me + k, owners)
            pltpu.make_async_remote_copy(
                source.at[peer], landing.at[me], send_sem, recv_sem,
                device_id=(rep, peer), device_id_type=MESH,
            ).start()
            return carry

        lax.fori_loop(1, owners, send, 0)
        return pltpu.make_async_remote_copy(
            source.at[pl.ds(0, owners - 1)], landing.at[pl.ds(0, owners - 1)], send_sem, recv_sem,
            device_id=(rep, lax.rem(me + 1, owners)), device_id_type=MESH,
        )

    arriving = []
    for c in range(CHUNKS):
        for copy in gossip[c]:
            copy.wait_recv()
        delta = (
            from_left[c].astype(jnp.float32)
            + from_right[c].astype(jnp.float32)
            - 2.0 * message[c].astype(jnp.float32)
        )
        mixed[c] = (tracker[:, :, span(c)].astype(jnp.float32) + gamma_mix * delta).astype(jnp.bfloat16)
        arriving.append(exchange(mixed.at[c], held.at[c], in_send.at[c], in_recv.at[c]))
        held[c, me] = mixed[c, me]

    gram = jnp.zeros((rows, rows), jnp.float32)
    for c in range(CHUNKS):
        arriving[c].wait_recv()
        block = held[c].reshape(rows, width)
        gram += lax.dot_general(
            block, block, (((1,), (1,)), ((), ())), preferred_element_type=jnp.float32
        )
    factor = newton_schulz_factor(gram, columns).astype(jnp.bfloat16)

    leaving = []
    for c in range(CHUNKS):
        block = held[c].reshape(rows, width)
        update = jnp.dot(factor, block, preferred_element_type=jnp.float32).astype(jnp.bfloat16)
        done[c] = update.reshape(owners, 2, width)
        leaving.append(exchange(done.at[c], out.at[:, :, span(c)], out_send.at[c], out_recv.at[c]))
        out[me, :, span(c)] = done[c, me]

    for c in range(CHUNKS):
        for copy in gossip[c]:
            copy.wait_send()
        arriving[c].wait_send()
    for c in range(CHUNKS):
        leaving[c].wait()


def per_device(reps, owners, tracker, levels, exponents):
    blocks, rows, columns = tracker.shape[1:]
    powers = jnp.exp2(exponents.astype(jnp.float32)).astype(jnp.bfloat16)[0, :, :, None]
    width = columns // CHUNKS
    chunked = pltpu.VMEM((CHUNKS, blocks, rows, width), jnp.bfloat16)
    dma = pltpu.SemaphoreType.DMA
    result = pl.pallas_call(
        functools.partial(kernel, reps, owners, columns),
        out_shape=jax.ShapeDtypeStruct((blocks, rows, columns), jnp.bfloat16),
        in_specs=[pl.BlockSpec(memory_space=pltpu.VMEM)] * 3,
        out_specs=pl.BlockSpec(memory_space=pltpu.VMEM),
        scratch_shapes=[chunked] * 6 + [
            dma((2, CHUNKS)), dma((2, CHUNKS)),
            dma((CHUNKS,)), dma((CHUNKS,)), dma((CHUNKS,)), dma((CHUNKS,)), dma,
        ],
        compiler_params=pltpu.CompilerParams(collective_id=0, has_side_effects=True),
        name="muon",
    )(tracker[0], levels[0], powers)
    return result[None]


def solution(mesh):
    in_specs = (P("rep", None, "fsdp", None), P("rep", None, "fsdp", None), P("rep", None, "fsdp"))
    out_specs = P("rep", None, "fsdp", None)
    step = functools.partial(per_device, mesh.shape["rep"], mesh.shape["fsdp"])
    return jax.shard_map(
        step, mesh=mesh, in_specs=in_specs, out_specs=out_specs, check_vma=False
    )
```

profile of v0, /device:TPU:1, one launch (start us, length us, event | category | flops | bytes accessed | tf_op | source)
XLA Modules:
  0.0 160.4 jit_solution(8167601173857104191)
XLA Ops:
  0.0 0.7 fusion
  0.7 0.7 copy.4.powers
  1.4 155.7 %muon.1 = bf16[64,2,5120]{2,1,0:T(2,128)(2,1)} custom-call(bf16[64,2,5120]{2,1,0:T(2,128)(2,1)} %bitcast.6, bf16[64,2,5120]{2,1,0:T(2,128)(2,1)} %bitcast.7, bf16[64,2,1]{2,1,0:T(2,128)(2,1)} %copy.4.powers), custom_call_target="tpu_custom_call" | custom-call | tf_op jit(solution)/shard_map/muon/pallas_call | solution.py:146
  157.2 3.3 %copy.6 = bf16[1,64,2,5120]{3,2,1,0:T(2,128)(2,1)} copy(bf16[1,64,2,5120]{3,2,1,0:T(2,128)(2,1)} %bitcast.5) | data formatting | bytes 2621440
where the time goes:
time: 161 us; the launch traced here: 160 us
  Pallas kernels  156 us (97%)
  local copies, waits for them, and re-layouts  4.02 us (2%)
    pallas_call x1, Pallas kernels, per_device(): pl.pallas_call(functools.partial(kernel, reps, owners, columns), out_shap...  156 us
    unnamed x1, local copies, waits for them, and re-layouts  3.27 us

commit v1 on v0

v1 whole, which is shorter than its diff:
```python
import functools
import math

import jax
import jax.numpy as jnp
from jax import lax
from jax.experimental import pallas as pl
from jax.experimental.pallas import tpu as pltpu
from jax.sharding import PartitionSpec as P

NS_STEPS = 5
MESH = pl.DeviceIdType.MESH
PIECES = (
    (0, 0, 256), (0, 256, 512), (0, 768, 768), (0, 1536, 1024),
    (1, 0, 1280), (1, 1280, 1280),
)
WAVES = 2

gamma_mix = 0.5
coef_a = 3.4445
coef_b = -4.775
coef_c = 2.0315


def dot32(a, b):
    return lax.dot_general(
        a, b, (((1,), (0,)), ((), ())),
        precision=lax.Precision.HIGHEST, preferred_element_type=jnp.float32,
    )


def newton_schulz_factor(gram, columns):
    size = gram.shape[0]
    row = lax.broadcasted_iota(jnp.int32, (size, size), 0)
    col = lax.broadcasted_iota(jnp.int32, (size, size), 1)
    eye = row == col
    total = jnp.sum(jnp.sum(jnp.where(eye, gram, 0.0), axis=1, keepdims=True), axis=0, keepdims=True)
    scale = 1.0 / (jnp.sqrt(total) + 1e-07)
    gram = (gram * scale) * scale
    factor = None
    for step in range(NS_STEPS):
        square = dot32(gram, gram)
        poly = jnp.where(eye, coef_a, 0.0) + coef_b * gram + coef_c * square
        factor = poly if factor is None else dot32(poly, factor)
        if step < NS_STEPS - 1:
            gram = dot32(dot32(poly, gram), poly)
    return factor * (scale * 2.0 ** (int(math.log2(columns)) // 2))


def powers_of_two(exponents):
    power = jnp.full(exponents.shape, 2.0**-8, jnp.float32)
    for reached in (-7, -6, -5):
        power = power * jnp.where(exponents >= reached, 2.0, 1.0)
    return power


def kernel(
    reps, owners, exponents, tracker, levels, out,
    held_tracker, held_levels, message, from_left, from_right, mixed, held, done, gram_own, gram_other,
    load_sem, gossip_send, gossip_recv, in_send, in_recv, out_send, out_recv, gram_send, gram_recv, rounds,
):
    rep, me = lax.axis_index("rep"), lax.axis_index("fsdp")
    after, before = lax.rem(rep + 1, reps), lax.rem(rep + reps - 1, reps)
    pair, half = lax.div(me, 2), lax.rem(me, 2)
    plane, seat = lax.div(me, 4), lax.rem(me, 4)
    partner = me + 1 - 2 * half
    pairs, width = owners // 2, held.shape[-1]
    rows = 2 * owners

    def planes_off(distance):
        return lax.rem(plane + distance + owners // 4, owners // 4) * 4

    loads = []
    for w in range(WAVES):
        for i, (source, landing) in enumerate(((levels, held_levels), (tracker, held_tracker))):
            copy = pltpu.make_async_copy(source.at[:, w], landing.at[w], load_sem.at[w, i])
            copy.start()
            loads.append(copy)

    barrier = pltpu.get_barrier_semaphore()
    for other in (before, after):
        pl.semaphore_signal(barrier, inc=1, device_id=(other, me), device_id_type=MESH)
    for j in range(1, 4):
        pl.semaphore_signal(
            barrier, inc=1, device_id=(rep, planes_off(0) + lax.rem(seat + j, 4)), device_id_type=MESH
        )
    for distance in (1, -1):
        for j in range(4):
            pl.semaphore_signal(
                barrier, inc=1, device_id=(rep, planes_off(distance) + j), device_id_type=MESH
            )

    powers = powers_of_two(exponents[...]).T.reshape(pairs, WAVES, 2, 1).astype(jnp.bfloat16)

    def gossip_copies(i):
        w, first, count = PIECES[i]
        span = pl.ds(first, count)
        return [
            pltpu.make_async_remote_copy(
                message.at[w, :, :, span], landing.at[w, :, :, span],
                gossip_send.at[side, i], gossip_recv.at[side, i],
                device_id=(other, me), device_id_type=MESH,
            )
            for side, (other, landing) in enumerate(((after, from_left), (before, from_right)))
        ]

    gossip = []
    for i, (w, first, count) in enumerate(PIECES):
        span = slice(first, first + count)
        if first == 0:
            loads[2 * w].wait()
        scaled = held_levels[w, :, :, :, span] * powers[:, w][:, None]
        message[w, :, :, span] = scaled.reshape(owners, 2, count)
        if i == 0:
            pl.semaphore_wait(barrier, 13)
        gossip.append(gossip_copies(i))
        for copy in gossip[i]:
            copy.start()

    for i, distance in enumerate((1, 2, 4)):
        for sign in (1, -1):
            pl.semaphore_signal(
                rounds.at[i], inc=1, device_id=(rep, planes_off(sign * distance) + seat),
                device_id_type=MESH,
            )
        pl.semaphore_wait(rounds.at[i], 2)

    def exchange(source, landing, send_sem, recv_sem):
        def send(k, carry):
            peer = lax.rem(me + k, owners)
            pltpu.make_async_remote_copy(
                source(peer), landing, send_sem, recv_sem, device_id=(rep, peer), device_id_type=MESH
            ).start()
            return carry

        lax.fori_loop(1, owners, send, 0)

    arriving = []
    for i, (w, first, count) in enumerate(PIECES):
        span, cut = pl.ds(first, count), slice(first, first + count)
        if first == 0:
            loads[2 * w + 1].wait()
        for copy in gossip[i]:
            copy.wait_recv()
        delta = (
            from_left[w, :, :, cut].astype(jnp.float32)
            + from_right[w, :, :, cut].astype(jnp.float32)
            - 2.0 * message[w, :, :, cut].astype(jnp.float32)
        )
        base = held_tracker[w, :, :, :, cut].reshape(owners, 2, count).astype(jnp.float32)
        mixed[w, :, :, cut] = (base + gamma_mix * delta).astype(jnp.bfloat16)
        exchange(
            lambda peer: mixed.at[w, peer, :, span], held.at[w, me, :, span], in_send.at[i], in_recv.at[i]
        )
        held[w, me, :, cut] = mixed[w, me, :, cut]
        arriving.append(
            pltpu.make_async_remote_copy(
                mixed.at[w, pl.ds(0, owners - 1), :, span], held.at[w, pl.ds(0, owners - 1), :, span],
                in_send.at[i], in_recv.at[i], device_id=(rep, partner), device_id_type=MESH,
            )
        )

    leaving = []
    for w in range(WAVES):
        gram = jnp.zeros((rows, rows), jnp.float32)
        for i, (wave, first, count) in enumerate(PIECES):
            if wave != w:
                continue
            arriving[i].wait_recv()
            block = held[w, :, :, first : first + count].reshape(rows, count)
            gram += lax.dot_general(
                block, block, (((1,), (1,)), ((), ())), preferred_element_type=jnp.float32
            )
        gram_own[w] = gram
        swap = pltpu.make_async_remote_copy(
            gram_own.at[w], gram_other.at[w], gram_send.at[w], gram_recv.at[w],
            device_id=(rep, partner), device_id_type=MESH,
        )
        swap.start()
        swap.wait()
        factor = newton_schulz_factor(gram_own[w] + gram_other[w], 2 * width).astype(jnp.bfloat16)
        update = jnp.dot(
            factor, held[w].reshape(rows, width), preferred_element_type=jnp.float32
        ).astype(jnp.bfloat16)
        done[w] = update.reshape(owners, 2, width)
        exchange(
            lambda peer: done.at[w, peer], out.at[pair, w, half], out_send.at[w], out_recv.at[w]
        )
        out[pair, w, half] = done[w, me]
        for wait_of in (out_send, out_recv):
            leaving.append((w, wait_of))

    for i in range(len(PIECES)):
        for copy in gossip[i]:
            copy.wait_send()
        arriving[i].wait_send()
    for w in range(WAVES):
        pltpu.make_async_remote_copy(
            done.at[w, pl.ds(0, owners - 1)], held.at[w, pl.ds(0, owners - 1)],
            out_send.at[w], out_recv.at[w], device_id=(rep, partner), device_id_type=MESH,
        ).wait()


def hand_out(source, out, sem):
    copy = pltpu.make_async_copy(source, out, sem)
    copy.start()
    copy.wait()


def halves(array):
    _, blocks, rows, columns = array.shape
    return array.reshape(blocks // 2, 2, rows, 2, columns // 2).transpose(0, 1, 3, 2, 4)


def per_device(reps, owners, tracker, levels, exponents):
    _, blocks, rows, columns = tracker.shape
    split = (blocks // 2, 2, 2, rows, columns // 2)
    half = (WAVES, blocks, rows, columns // 2)
    by_wave = pltpu.VMEM((WAVES, blocks // 2, 2, rows, columns // 2), jnp.bfloat16)
    dma = pltpu.SemaphoreType.DMA
    pieces = len(PIECES)
    result = pl.pallas_call(
        functools.partial(kernel, reps, owners),
        out_shape=pltpu.VMEM(split, jnp.bfloat16),
        in_specs=[pl.BlockSpec(memory_space=pltpu.VMEM)] + [pl.BlockSpec(memory_space=pl.ANY)] * 2,
        out_specs=pl.BlockSpec(memory_space=pltpu.VMEM),
        scratch_shapes=[by_wave] * 2 + [pltpu.VMEM(half, jnp.bfloat16)] * 6
        + [pltpu.VMEM((WAVES, 2 * owners, 2 * owners), jnp.float32)] * 2
        + [
            dma((WAVES, 2)), dma((2, pieces)), dma((2, pieces)), dma((pieces,)), dma((pieces,)),
            dma((WAVES,)), dma((WAVES,)), dma((WAVES,)), dma((WAVES,)), pltpu.SemaphoreType.REGULAR((3,)),
        ],
        compiler_params=pltpu.CompilerParams(collective_id=0, has_side_effects=True),
        name="muon",
    )(exponents[0].T, halves(tracker), halves(levels))
    result = pl.pallas_call(
        hand_out,
        out_shape=jax.ShapeDtypeStruct(split, jnp.bfloat16),
        in_specs=[pl.BlockSpec(memory_space=pltpu.VMEM)],
        out_specs=pl.BlockSpec(memory_space=pl.ANY),
        scratch_shapes=[dma],
        name="hand_out",
    )(pltpu.with_memory_space_constraint(result, pltpu.VMEM))
    return result.transpose(0, 1, 3, 2, 4).reshape(1, blocks, rows, columns)


def solution(mesh):
    in_specs = (P("rep", None, "fsdp", None), P("rep", None, "fsdp", None), P("rep", None, "fsdp"))
    out_specs = P("rep", None, "fsdp", None)
    step = functools.partial(per_device, mesh.shape["rep"], mesh.shape["fsdp"])
    return jax.shard_map(
        step, mesh=mesh, in_specs=in_specs, out_specs=out_specs, check_vma=False
    )
```

time: 161 us -> 140 us (0.87)
  Pallas kernels: 156 us -> 139 us
  local copies, waits for them, and re-layouts: 4.02 us -> 0 us
    pallas_call x1 -> x2, Pallas kernels: 156 us -> 139 us  [the longest x1 138 us: per_device(): pl.pallas_call(functools.partial(kernel, reps, owners), out_shape=pltpu.V...]
    unnamed x1 -> x0, local copies, waits for them, and re-layouts: 3.27 us -> none
where the time goes in v1:
time: 140 us; the launch traced here: 139 us
  Pallas kernels  139 us (99%)
    pallas_call x1, Pallas kernels, per_device(): pl.pallas_call(functools.partial(kernel, reps, owners), out_shape=pltpu.V...  138 us

profile of v1, /device:TPU:1, one launch (start us, length us, event | category | flops | bytes accessed | tf_op | source)
XLA Modules:
  0.0 139.5 jit_solution(2064168582900568245)
XLA Ops:
  0.0 138.4 %muon.1.source = bf16[32,2,2,2,2560]{4,3,2,1,0:T(2,128)(2,1)S(1)} custom-call(s32[2,64]{1,0:T(2,128)} %bitcast.14, bf16[32,2,2,2,2560]{4,3,2,1,0:T(2,128)(2,1)} %bitcast.12, bf16[32,2,2,2,2560]{4,3,2,1,0:T(2,128)(2,1)} %bitcast.13), custom_call_target="tpu_custom_call" | custom-call | tf_op jit(solution)/shard_map/muon/pallas_call | solution.py:222
  138.4 1.1 hand_out.1

commit v2 on v1

--- a/solution.py
+++ b/solution.py
@@ -11,10 +11,14 @@
 NS_STEPS = 5
 MESH = pl.DeviceIdType.MESH
 PIECES = (
-    (0, 0, 256), (0, 256, 512), (0, 768, 768), (0, 1536, 1024),
+    (0, 0, 128), (0, 128, 256), (0, 384, 512), (0, 896, 768), (0, 1664, 896),
     (1, 0, 1280), (1, 1280, 1280),
 )
 WAVES = 2
+NEAR = (2, -2, 1, -1)
+ROUNDS = (2, 4)
+ORDER = (8, 7, 6, 5, 4, 3, 2, 1, 0)
+FIRST_NEAR, FIRST_FAR = (4, 3, 2, 1, 0), (8, 7, 6, 5)
 
 gamma_mix = 0.5
 coef_a = 3.4445
@@ -56,8 +60,8 @@
 
 def kernel(
     reps, owners, exponents, tracker, levels, out,
-    held_tracker, held_levels, message, from_left, from_right, mixed, held, done, gram_own, gram_other,
-    load_sem, gossip_send, gossip_recv, in_send, in_recv, out_send, out_recv, gram_send, gram_recv, rounds,
+    held_exponents, held_tracker, held_levels, message, from_left, from_right, mixed, held, done, gram_own, gram_other,
+    exponents_sem, load_sem, gossip_send, gossip_recv, in_send, in_recv, out_send, out_recv, gram_send, gram_recv, rounds,
 ):
     rep, me = lax.axis_index("rep"), lax.axis_index("fsdp")
     after, before = lax.rem(rep + 1, reps), lax.rem(rep + reps - 1, reps)
@@ -70,6 +74,21 @@
     def planes_off(distance):
         return lax.rem(plane + distance + owners // 4, owners // 4) * 4
 
+    barrier = pltpu.get_barrier_semaphore()
+    for other in (before, after):
+        pl.semaphore_signal(barrier, inc=1, device_id=(other, me), device_id_type=MESH)
+    for j in range(1, 4):
+        pl.semaphore_signal(
+            barrier, inc=1, device_id=(rep, planes_off(0) + lax.rem(seat + j, 4)), device_id_type=MESH
+        )
+    for distance in NEAR:
+        for j in range(4):
+            pl.semaphore_signal(
+                barrier, inc=1, device_id=(rep, planes_off(distance) + j), device_id_type=MESH
+            )
+
+    exponents_load = pltpu.make_async_copy(exponents, held_exponents, exponents_sem)
+    exponents_load.start()
     loads = []
     for w in range(WAVES):
         for i, (source, landing) in enumerate(((levels, held_levels), (tracker, held_tracker))):
@@ -77,20 +96,8 @@
             copy.start()
             loads.append(copy)
 
-    barrier = pltpu.get_barrier_semaphore()
-    for other in (before, after):
-        pl.semaphore_signal(barrier, inc=1, device_id=(other, me), device_id_type=MESH)
-    for j in range(1, 4):
-        pl.semaphore_signal(
-            barrier, inc=1, device_id=(rep, planes_off(0) + lax.rem(seat + j, 4)), device_id_type=MESH
-        )
-    for distance in (1, -1):
-        for j in range(4):
-            pl.semaphore_signal(
-                barrier, inc=1, device_id=(rep, planes_off(distance) + j), device_id_type=MESH
-            )
-
-    powers = powers_of_two(exponents[...]).T.reshape(pairs, WAVES, 2, 1).astype(jnp.bfloat16)
+    exponents_load.wait()
+    powers = powers_of_two(held_exponents[...]).T.reshape(pairs, WAVES, 2, 1).astype(jnp.bfloat16)
 
     def gossip_copies(i):
         w, first, count = PIECES[i]
@@ -112,28 +119,34 @@
         scaled = held_levels[w, :, :, :, span] * powers[:, w][:, None]
         message[w, :, :, span] = scaled.reshape(owners, 2, count)
         if i == 0:
-            pl.semaphore_wait(barrier, 13)
+            pl.semaphore_wait(barrier, 5 + 4 * len(NEAR))
         gossip.append(gossip_copies(i))
         for copy in gossip[i]:
             copy.start()
 
-    for i, distance in enumerate((1, 2, 4)):
+    def tell(i):
         for sign in (1, -1):
             pl.semaphore_signal(
-                rounds.at[i], inc=1, device_id=(rep, planes_off(sign * distance) + seat),
+                rounds.at[i], inc=1, device_id=(rep, planes_off(sign * ROUNDS[i]) + seat),
                 device_id_type=MESH,
             )
-        pl.semaphore_wait(rounds.at[i], 2)
-
-    def exchange(source, landing, send_sem, recv_sem):
-        def send(k, carry):
-            peer = lax.rem(me + k, owners)
+
+    tell(0)
+    pl.semaphore_wait(rounds.at[0], 2)
+    tell(1)
+
+    def exchange(source, landing, send_sem, recv_sem, distances):
+        def send(peer):
             pltpu.make_async_remote_copy(
                 source(peer), landing, send_sem, recv_sem, device_id=(rep, peer), device_id_type=MESH
             ).start()
-            return carry
-
-        lax.fori_loop(1, owners, send, 0)
+
+        for distance in distances:
+            for j in range(0 if distance else 1, 4):
+                to = lax.rem(seat + j, 4)
+                send(planes_off(distance) + to)
+                if 0 < distance < 8:
+                    send(planes_off(-distance) + to)
 
     arriving = []
     for i, (w, first, count) in enumerate(PIECES):
@@ -149,9 +162,16 @@
         )
         base = held_tracker[w, :, :, :, cut].reshape(owners, 2, count).astype(jnp.float32)
         mixed[w, :, :, cut] = (base + gamma_mix * delta).astype(jnp.bfloat16)
-        exchange(
-            lambda peer: mixed.at[w, peer, :, span], held.at[w, me, :, span], in_send.at[i], in_recv.at[i]
-        )
+        send_piece = functools.partial(
+            exchange, lambda peer: mixed.at[w, peer, :, span], held.at[w, me, :, span],
+            in_send.at[i], in_recv.at[i],
+        )
+        if i == 0:
+            send_piece(FIRST_NEAR)
+            pl.semaphore_wait(rounds.at[1], 2)
+            send_piece(FIRST_FAR)
+        else:
+            send_piece(ORDER)
         held[w, me, :, cut] = mixed[w, me, :, cut]
         arriving.append(
             pltpu.make_async_remote_copy(
@@ -160,7 +180,6 @@
             )
         )
 
-    leaving = []
     for w in range(WAVES):
         gram = jnp.zeros((rows, rows), jnp.float32)
         for i, (wave, first, count) in enumerate(PIECES):
@@ -184,11 +203,9 @@
         ).astype(jnp.bfloat16)
         done[w] = update.reshape(owners, 2, width)
         exchange(
-            lambda peer: done.at[w, peer], out.at[pair, w, half], out_send.at[w], out_recv.at[w]
+            lambda peer: done.at[w, peer], out.at[pair, w, half], out_send.at[w], out_recv.at[w], ORDER
         )
         out[pair, w, half] = done[w, me]
-        for wait_of in (out_send, out_recv):
-            leaving.append((w, wait_of))
 
     for i in range(len(PIECES)):
         for copy in gossip[i]:
@@ -202,9 +219,16 @@
 
 
 def hand_out(source, out, sem):
-    copy = pltpu.make_async_copy(source, out, sem)
-    copy.start()
-    copy.wait()
+    parts = sem.shape[0]
+    count = source.shape[0] // parts
+    copies = [
+        pltpu.make_async_copy(source.at[pl.ds(i * count, count)], out.at[pl.ds(i * count, count)], sem.at[i])
+        for i in range(parts)
+    ]
+    for copy in copies:
+        copy.start()
+    for copy in copies:
+        copy.wait()
 
 
 def halves(array):
@@ -222,13 +246,13 @@
     result = pl.pallas_call(
         functools.partial(kernel, reps, owners),
         out_shape=pltpu.VMEM(split, jnp.bfloat16),
-        in_specs=[pl.BlockSpec(memory_space=pltpu.VMEM)] + [pl.BlockSpec(memory_space=pl.ANY)] * 2,
+        in_specs=[pl.BlockSpec(memory_space=pl.ANY)] * 3,
         out_specs=pl.BlockSpec(memory_space=pltpu.VMEM),
-        scratch_shapes=[by_wave] * 2 + [pltpu.VMEM(half, jnp.bfloat16)] * 6
+        scratch_shapes=[pltpu.VMEM((rows, blocks), jnp.int32)] + [by_wave] * 2 + [pltpu.VMEM(half, jnp.bfloat16)] * 6
         + [pltpu.VMEM((WAVES, 2 * owners, 2 * owners), jnp.float32)] * 2
         + [
-            dma((WAVES, 2)), dma((2, pieces)), dma((2, pieces)), dma((pieces,)), dma((pieces,)),
-            dma((WAVES,)), dma((WAVES,)), dma((WAVES,)), dma((WAVES,)), pltpu.SemaphoreType.REGULAR((3,)),
+            dma, dma((WAVES, 2)), dma((2, pieces)), dma((2, pieces)), dma((pieces,)), dma((pieces,)),
+            dma((WAVES,)), dma((WAVES,)), dma((WAVES,)), dma((WAVES,)), pltpu.SemaphoreType.REGULAR((len(ROUNDS),)),
         ],
         compiler_params=pltpu.CompilerParams(collective_id=0, has_side_effects=True),
         name="muon",
@@ -238,7 +262,7 @@
         out_shape=jax.ShapeDtypeStruct(split, jnp.bfloat16),
         in_specs=[pl.BlockSpec(memory_space=pltpu.VMEM)],
         out_specs=pl.BlockSpec(memory_space=pl.ANY),
-        scratch_shapes=[dma],
+        scratch_shapes=[dma((8,))],
         name="hand_out",
     )(pltpu.with_memory_space_constraint(result, pltpu.VMEM))
     return result.transpose(0, 1, 3, 2, 4).reshape(1, blocks, rows, columns)

time: 140 us -> 138 us (0.986)
    pallas_call x1, Pallas kernels: 138 us -> 137 us  [per_device(): pl.pallas_call(functools.partial(kernel, reps, owners), out_shape=pltpu.V...]
where the time goes in v2:
time: 138 us
  Pallas kernels  138 us (100%)
    pallas_call x1, Pallas kernels, per_device(): pl.pallas_call(functools.partial(kernel, reps, owners), out_shape=pltpu.V...  137 us

profile of v2, /device:TPU:1, one launch (start us, length us, event | category | flops | bytes accessed | tf_op | source)
XLA Modules:
  0.0 137.7 jit_solution(3090395532177787562)
XLA Ops:
  0.0 136.6 %muon.1.source = bf16[32,2,2,2,2560]{4,3,2,1,0:T(2,128)(2,1)S(1)} custom-call(s32[2,64]{1,0:T(2,128)} %bitcast.14, bf16[32,2,2,2,2560]{4,3,2,1,0:T(2,128)(2,1)} %bitcast.12, bf16[32,2,2,2,2560]{4,3,2,1,0:T(2,128)(2,1)} %bitcast.13), custom_call_target="tpu_custom_call" | custom-call | tf_op jit(solution)/shard_map/muon/pallas_call | solution.py:246
  136.6 1.1 hand_out.1

commit v3 on v2

--- a/solution.py
+++ b/solution.py
@@ -18,6 +18,7 @@
 NEAR = (2, -2, 1, -1)
 ROUNDS = (2, 4)
 ORDER = (8, 7, 6, 5, 4, 3, 2, 1, 0)
+SERVED_FIRST = ((0, 3), (15, 7))
 FIRST_NEAR, FIRST_FAR = (4, 3, 2, 1, 0), (8, 7, 6, 5)
 
 gamma_mix = 0.5
@@ -61,7 +62,7 @@
 def kernel(
     reps, owners, exponents, tracker, levels, out,
     held_exponents, held_tracker, held_levels, message, from_left, from_right, mixed, held, done, gram_own, gram_other,
-    exponents_sem, load_sem, gossip_send, gossip_recv, in_send, in_recv, out_send, out_recv, gram_send, gram_recv, rounds,
+    exponents_sem, load_sem, gossip_send, gossip_recv, in_send, in_recv, out_send, out_recv, gram_send, gram_recv, own_sem, rounds,
 ):
     rep, me = lax.axis_index("rep"), lax.axis_index("fsdp")
     after, before = lax.rem(rep + 1, reps), lax.rem(rep + reps - 1, reps)
@@ -135,18 +136,39 @@
     pl.semaphore_wait(rounds.at[0], 2)
     tell(1)
 
-    def exchange(source, landing, send_sem, recv_sem, distances):
+    def exchange(source, landing, send_sem, recv_sem, distances, levels_of_planes=()):
         def send(peer):
             pltpu.make_async_remote_copy(
                 source(peer), landing, send_sem, recv_sem, device_id=(rep, peer), device_id_type=MESH
             ).start()
 
-        for distance in distances:
+        def send_plane(distance, signs):
             for j in range(0 if distance else 1, 4):
                 to = lax.rem(seat + j, 4)
-                send(planes_off(distance) + to)
-                if 0 < distance < 8:
-                    send(planes_off(-distance) + to)
+                for sign in signs:
+                    send(planes_off(sign * distance) + to)
+
+        def both(distance):
+            return (1, -1) if 0 < distance < 8 else (1,)
+
+        if not levels_of_planes:
+            for distance in distances:
+                send_plane(distance, both(distance))
+            return
+
+        def within(distance, sign, first, count):
+            there = lax.div(planes_off(sign * distance), 4)
+            return lax.rem(there + owners // 4 - first, owners // 4) < count
+
+        before = None
+        for level in levels_of_planes + (None,):
+            for distance in distances:
+                for sign in both(distance):
+                    now = None if level is None else within(distance, sign, *level)
+                    past = None if before is None else jnp.logical_not(within(distance, sign, *before))
+                    pred = past if now is None else now if past is None else jnp.logical_and(now, past)
+                    pl.when(pred)(functools.partial(send_plane, distance, (sign,)))
+            before = level
 
     arriving = []
     for i, (w, first, count) in enumerate(PIECES):
@@ -180,6 +202,7 @@
             )
         )
 
+    kept = []
     for w in range(WAVES):
         gram = jnp.zeros((rows, rows), jnp.float32)
         for i, (wave, first, count) in enumerate(PIECES):
@@ -203,14 +226,19 @@
         ).astype(jnp.bfloat16)
         done[w] = update.reshape(owners, 2, width)
         exchange(
-            lambda peer: done.at[w, peer], out.at[pair, w, half], out_send.at[w], out_recv.at[w], ORDER
-        )
-        out[pair, w, half] = done[w, me]
+            lambda peer: done.at[w, peer], out.at[pair, w, half], out_send.at[w], out_recv.at[w], ORDER,
+            SERVED_FIRST if w == WAVES - 1 else (),
+        )
+        own = pltpu.make_async_copy(done.at[w, me], out.at[pair, w, half], own_sem.at[w])
+        own.start()
+        kept.append(own)
 
     for i in range(len(PIECES)):
         for copy in gossip[i]:
             copy.wait_send()
         arriving[i].wait_send()
+    for own in kept:
+        own.wait()
     for w in range(WAVES):
         pltpu.make_async_remote_copy(
             done.at[w, pl.ds(0, owners - 1)], held.at[w, pl.ds(0, owners - 1)],
@@ -247,12 +275,12 @@
         functools.partial(kernel, reps, owners),
         out_shape=pltpu.VMEM(split, jnp.bfloat16),
         in_specs=[pl.BlockSpec(memory_space=pl.ANY)] * 3,
-        out_specs=pl.BlockSpec(memory_space=pltpu.VMEM),
+        out_specs=pl.BlockSpec(memory_space=pl.ANY),
         scratch_shapes=[pltpu.VMEM((rows, blocks), jnp.int32)] + [by_wave] * 2 + [pltpu.VMEM(half, jnp.bfloat16)] * 6
         + [pltpu.VMEM((WAVES, 2 * owners, 2 * owners), jnp.float32)] * 2
         + [
             dma, dma((WAVES, 2)), dma((2, pieces)), dma((2, pieces)), dma((pieces,)), dma((pieces,)),
-            dma((WAVES,)), dma((WAVES,)), dma((WAVES,)), dma((WAVES,)), pltpu.SemaphoreType.REGULAR((len(ROUNDS),)),
+            dma((WAVES,)), dma((WAVES,)), dma((WAVES,)), dma((WAVES,)), dma((WAVES,)), pltpu.SemaphoreType.REGULAR((len(ROUNDS),)),
         ],
         compiler_params=pltpu.CompilerParams(collective_id=0, has_side_effects=True),
         name="muon",

time: 138 us -> 135 us (0.978); the launches traced: 138 us -> 133 us
  Pallas kernels: 138 us -> 133 us
    pallas_call x1, Pallas kernels: 137 us -> 132 us  [per_device(): pl.pallas_call(functools.partial(kernel, reps, owners), out_shape=pltpu.V...]
where the time goes in v3:
time: 135 us; the launch traced here: 133 us
  Pallas kernels  133 us (99%)
    pallas_call x1, Pallas kernels, per_device(): pl.pallas_call(functools.partial(kernel, reps, owners), out_shape=pltpu.V...  132 us

profile of v3, /device:TPU:1, one launch (start us, length us, event | category | flops | bytes accessed | tf_op | source)
XLA Modules:
  0.0 133.2 jit_solution(6356125999215153076)
XLA Ops:
  0.0 132.0 %muon.1.source = bf16[32,2,2,2,2560]{4,3,2,1,0:T(2,128)(2,1)S(1)} custom-call(s32[2,64]{1,0:T(2,128)} %bitcast.14, bf16[32,2,2,2,2560]{4,3,2,1,0:T(2,128)(2,1)} %bitcast.12, bf16[32,2,2,2,2560]{4,3,2,1,0:T(2,128)(2,1)} %bitcast.13), custom_call_target="tpu_custom_call" | custom-call | tf_op jit(solution)/shard_map/muon/pallas_call | solution.py:274
  132.0 1.1 hand_out.1

commit v4 on v3

--- a/solution.py
+++ b/solution.py
@@ -11,8 +11,8 @@
 NS_STEPS = 5
 MESH = pl.DeviceIdType.MESH
 PIECES = (
-    (0, 0, 128), (0, 128, 256), (0, 384, 512), (0, 896, 768), (0, 1664, 896),
-    (1, 0, 1280), (1, 1280, 1280),
+    (0, 0, 128), (0, 128, 256), (0, 384, 384), (0, 768, 512), (0, 1280, 640), (0, 1920, 640),
+    (1, 0, 640), (1, 640, 896), (1, 1536, 1024),
 )
 WAVES = 2
 NEAR = (2, -2, 1, -1)
@@ -162,7 +162,7 @@
 
         before = None
         for level in levels_of_planes + (None,):
-            for distance in distances:
+            for distance in distances[::-1] if level == levels_of_planes[0] else distances:
                 for sign in both(distance):
                     now = None if level is None else within(distance, sign, *level)
                     past = None if before is None else jnp.logical_not(within(distance, sign, *before))

time: 135 us -> 135 us (level)
  the two profiles are of different devices: /device:TPU:1 before, /device:TPU:193 now
where the time goes in v4:
time: 135 us
  Pallas kernels  135 us (100%)
    pallas_call x1, Pallas kernels, per_device(): pl.pallas_call(functools.partial(kernel, reps, owners), out_shape=pltpu.V...  134 us

profile of v4, /device:TPU:193, one launch (start us, length us, event | category | flops | bytes accessed | tf_op | source)
XLA Modules:
  0.0 135.0 jit_solution(13329961499214522508)
XLA Ops:
  0.0 133.8 %muon.1.source = bf16[32,2,2,2,2560]{4,3,2,1,0:T(2,128)(2,1)S(1)} custom-call(s32[2,64]{1,0:T(2,128)} %bitcast.14, bf16[32,2,2,2,2560]{4,3,2,1,0:T(2,128)(2,1)} %bitcast.12, bf16[32,2,2,2,2560]{4,3,2,1,0:T(2,128)(2,1)} %bitcast.13), custom_call_target="tpu_custom_call" | custom-call | tf_op jit(solution)/shard_map/muon/pallas_call | solution.py:274
  133.8 1.1 hand_out.1
